TPU v7x, 32 devices: a whole 2x2x4 slice. The times are simulated.
32 devices in a mesh: kf: 8 (over z, y), kc: 4 (over x, core).
Axes of the slice: x: 2, y: 2, z: 4, core: 2. Of those that a mesh axis runs over, the one named last changes fastest.
Arguments:
- kernel_coarse: bfloat16 [256, 256], P('kf'), may hold values from -6 to 6
- coefficients: bfloat16 [128, 256], P(('kf', 'kc')), may hold values from -1.5 to 1.5
- nearest: int32 [128], replicated, may hold values from 0 to 15
Outputs:
- kernel_fine: bfloat16 [2048, 2048], P('kf', 'kc')
All inputs are finite; a program needn't handle non-finite values.
Results may differ from a plain program's by a relative error of at most 0.0049.
Values may be sent and summed in bfloat16 or wider, within the bound.
A program may use at most 64 MiB of HBM per device.

v0:
```python
import jax
import jax.numpy as jnp
from jax import lax
from jax.sharding import PartitionSpec as P

P_SIZE = 16


def rotate(kernel_rows, coef_block):
    point_count = coef_block.shape[0]
    pair_count = coef_block.shape[1]
    shaped = kernel_rows.reshape(kernel_rows.shape[0], point_count, pair_count)
    turned = jnp.einsum("ckn,kan->cka", shaped, coef_block, preferred_element_type=jnp.float32)
    return turned.astype(jnp.bfloat16).reshape(kernel_rows.shape[0], point_count * pair_count)


def shards(kernel_coarse, coefficients, nearest):
    pair_count = P_SIZE
    total_rows = kernel_coarse.shape[1]
    fine_total = nearest.shape[0]
    slab_size = fine_total // lax.axis_size("kf")
    kc_count = lax.axis_size("kc")
    part_index = lax.axis_index("kc")
    offsets = jnp.arange(pair_count, dtype=jnp.int32)
    coef_whole = lax.all_gather(coefficients, ("kf", "kc"), axis=0, tiled=True).reshape(
        fine_total, pair_count, pair_count
    )
    share_size = slab_size // kc_count
    grouped = nearest.reshape(lax.axis_size("kf"), kc_count, share_size)
    chosen = lax.dynamic_index_in_dim(grouped, part_index, 1, keepdims=False)
    columns = (chosen.reshape(-1)[:, None] * pair_count + offsets[None, :]).reshape(-1)
    outgoing = jnp.take(kernel_coarse, columns, axis=1)
    received = lax.all_to_all(outgoing, "kf", split_axis=1, concat_axis=0, tiled=True)
    own_coef = coefficients.reshape(share_size, pair_count, pair_count)
    turned = rotate(received, own_coef)
    rotated = lax.all_gather(turned, "kc", axis=1, tiled=True)
    col_total = fine_total // kc_count
    col_coarse = lax.dynamic_slice_in_dim(nearest, part_index * col_total, col_total)
    coef_cols = lax.dynamic_slice_in_dim(coef_whole, part_index * col_total, col_total, 0)
    stacked = rotated.reshape(total_rows // pair_count, pair_count, rotated.shape[1])
    picked = jnp.take(stacked, col_coarse, axis=0)
    result = jnp.einsum("jnr,jbn->rjb", picked, coef_cols, preferred_element_type=jnp.float32)
    return result.reshape(result.shape[0], col_total * pair_count).astype(jnp.bfloat16)


def solution(mesh):
    in_specs = (P("kf", None), P(("kf", "kc"), None), P())
    out_specs = P("kf", "kc")
    return jax.shard_map(shards, mesh=mesh, in_specs=in_specs, out_specs=out_specs, check_vma=False)
```

profile of v0, /device:TPU:0, one launch (start us, length us, event | category | flops | bytes accessed | tf_op | source)
XLA Modules:
  0.0 63.8 jit_solution(2334305354638408349)
XLA Ops:
  0.0 0.7 %copy-done.2 = s32[128]{0:T(128)S(1)} copy-done((s32[128]{0:T(128)S(1)}, s32[128]{0:T(128)}, u32[]{:S(2)}) %copy-start.2) | copy-done | bytes 536
  0.7 0.1 reshape.90
  0.8 0.5 broadcast.58
  1.3 0.7 %fusion.6 = (s32[8,4]{1,0:T(8,128)S(1)}, s32[8,1,4]{2,1,0:T(1,128)S(1)}) fusion(s32[]{:T(128)} %broadcast.58, s32[8,4,4]{2,1,0:T(4,128)S(1)} %reshape.90, s32[]{:T(128)S(6)} %select_n.41), kind=kLoop, calls=%fused_computation.20 | loop fusion | flops 32 | bytes 392 | tf_op jit(solution)/shard_map/mul | solution.py:31
  2.0 0.1 mul.23
  2.0 0.1 add.82
  2.1 0.1 add.83
  2.2 0.1 iota_add_fusion
  2.3 0.1 add.92
  2.4 0.0 copy-start
  2.4 0.1 add.85
  2.5 0.6 copy-done
  3.1 0.1 copy.17
  3.2 1.3 %gather_fusion = bf16[512,32]{1,0:T(8,128)(2,1)S(1)} fusion(bf16[32,256]{0,1:T(8,128)(2,1)S(1)} %copy.17, s32[1024]{0:T(1024)S(1)} %pad_clamp_fusion.1), kind=kCustom, calls=%fused_computation | custom fusion | bytes 67584 | tf_op jit(solution)/shard_map/jit(_take)/gather | solution.py:32
  4.6 0.1 copy.18
  4.7 0.7 %reshape.124 = bf16[8,2,1024]{2,1,0:T(2,128)(2,1)} reshape(bf16[8,32,64]{2,1,0:T(8,128)(2,1)S(1)} %fusion.7) | data formatting | bytes 65536
  5.4 7.3 %all-to-all-start = ((bf16[8,2,1024]{2,1,0:T(2,128)(2,1)}), bf16[8,2,1024]{2,1,0:T(2,128)(2,1)S(1)}, u32[]{:S(2)}, u32[]{:S(2)}) async-start(bf16[8,2,1024]{2,1,0:T(2,128)(2,1)} %reshape.124), calls=%async_computation | async-start | bytes 65536 | tf_op jit(solution)/shard_map/all_to_all | solution.py:33
  12.8 0.1 compare_and_fusion.1
  12.8 0.6 copy-done.1
  13.4 0.1 reshape.92
  13.5 42.1 %all-gather = bf16[32,4,256]{2,1,0:T(4,128)(2,1)S(1)} all-gather(bf16[1,4,256]{2,1,0:T(4,128)(2,1)S(1)} %bitcast.28), channel_id=1, replica_groups=mesh['kf'=8,'kc'=4] {'kf','kc'}, dimensions={0}, use_global_device_ids=true | all-gather | bytes 67584 | tf_op jit(solution)/shard_map/all_gather | solution.py:25
  55.6 0.4 reshape.89
  56.0 0.0 all-to-all-done
  56.0 0.1 reshape.125
  56.1 0.1 copy.19
  56.3 0.1 reshape.91
  56.4 0.1 convolution_convert_fusion.1
  56.5 5.4 %all_gather.7 = bf16[256,256]{0,1:T(8,128)(2,1)S(1)} all-gather(bf16[256,64]{0,1:T(8,128)(2,1)S(1)} %bitcast.26), channel_id=1, replica_groups=mesh['kf'=8,'kc'=4] {'kc'}, dimensions={1}, use_global_device_ids=true | all-gather | bytes 163840 | tf_op jit(solution)/shard_map/all_gather | solution.py:36
  61.9 0.1 copy.20
  62.1 0.6 gather_fusion.1
  62.6 0.3 convolution_convert_fusion
  62.9 0.8 %copy.21 = bf16[256,512]{1,0:T(8,128)(2,1)} copy(bf16[256,512]{0,1:T(8,128)(2,1)S(1)} %bitcast.24) | data formatting | bytes 524288 | tf_op jit(solution)/shard_map/convert_element_type | solution.py:43
  (9 shorter events, 0.1 us)
Async XLA Ops:
  0.0 0.7 %copy-start.2 = (s32[128]{0:T(128)S(1)}, s32[128]{0:T(128)}, u32[]{:S(2)}) copy-start(s32[128]{0:T(128)} %param.5) | copy-start | bytes 1540
  2.4 0.7 %copy-start = (bf16[32,256]{1,0:T(8,128)(2,1)S(1)}, bf16[32,256]{1,0:T(8,128)(2,1)}, u32[]{:S(2)}) copy-start(bf16[32,256]{1,0:T(8,128)(2,1)} %param.3) | copy-start | bytes 49156
  5.4 50.6 %all-to-all-start = ((bf16[8,2,1024]{2,1,0:T(2,128)(2,1)}), bf16[8,2,1024]{2,1,0:T(2,128)(2,1)S(1)}, u32[]{:S(2)}, u32[]{:S(2)}) async-start(bf16[8,2,1024]{2,1,0:T(2,128)(2,1)} %reshape.124), calls=%async_computation | async-start | bytes 65536 | tf_op jit(solution)/shard_map/all_to_all | solution.py:33
  12.8 0.7 %copy-start.1 = (bf16[4,256]{1,0:T(4,128)(2,1)S(1)}, bf16[4,256]{1,0:T(4,128)(2,1)}, u32[]{:S(2)}) copy-start(bf16[4,256]{1,0:T(4,128)(2,1)} %param.4) | copy-start | bytes 6148
where the time goes:
time: 64.1 us; the launch traced here: 63.8 us
  blocking collectives  47.5 us (74%)
  local copies, waits for them, and re-layouts  7.54 us (12%)
  starting transfers between devices  7.31 us (11%)
  other arithmetic  0.86 us (1%)
    all_gather x1, blocking collectives, shards(): lax.all_gather(coefficients, ('kf', 'kc'), axis=0, tiled=True)  42.1 us
    all_to_all x1, starting transfers between devices, shards(): lax.all_to_all(outgoing, 'kf', split_axis=1, concat_axis=0, tiled=True)  7.31 us
    all_gather x1, blocking collectives, shards(): rotated = lax.all_gather(turned, 'kc', axis=1, tiled=True)  5.41 us
    unnamed x9, local copies, waits for them, and re-layouts  2.83 us
    gather x2, local copies, waits for them, and re-layouts, shards(): outgoing = jnp.take(kernel_coarse, columns, axis=1)  1.45 us
  transfers between devices with their start and end apart: 1, of which 0 were waited for; matrix products, arithmetic and copies ran while one was open for 1% of the time, Pallas kernels for 0%

commit v1 on v0

--- a/solution.py
+++ b/solution.py
@@ -33,7 +33,17 @@
     received = lax.all_to_all(outgoing, "kf", split_axis=1, concat_axis=0, tiled=True)
     own_coef = coefficients.reshape(share_size, pair_count, pair_count)
     turned = rotate(received, own_coef)
-    rotated = lax.all_gather(turned, "kc", axis=1, tiled=True)
+    p_count = lax.axis_size("kc")
+    big = turned
+    rows = [big]
+    out_arr = sorted(((m, (m + 1) % p_count) for m in range(p_count)))
+    for tick in tuple(range(1, p_count)):
+        big = lax.ppermute(big, "kc", out_arr)
+        rows.insert(0, big)
+    res = jnp.concatenate(rows, axis=1)
+    val = lax.axis_index("kc")
+    u_next = val + 1
+    rotated = jnp.roll(res, u_next * turned.shape[1], axis=1)
     col_total = fine_total // kc_count
     col_coarse = lax.dynamic_slice_in_dim(nearest, part_index * col_total, col_total)
     coef_cols = lax.dynamic_slice_in_dim(coef_whole, part_index * col_total, col_total, 0)

time: 64.1 us -> 68.4 us (1.067)
  waiting for transfers between devices: 0.01 us -> 13.2 us
  blocking collectives: 47.5 us -> 38.1 us
    ppermute x0 -> x3, waiting for transfers between devices: none -> 7.27 us  [shards(): big = lax.ppermute(big, 'kc', out_arr)]
    all_to_all x1, waiting for transfers between devices: 0.01 us -> 5.92 us  [shards(): lax.all_to_all(outgoing, 'kf', split_axis=1, concat_axis=0, tiled=True)]
    all_gather x1 -> x0, blocking collectives: 5.41 us -> none  [shards(): rotated = lax.all_gather(turned, 'kc', axis=1, tiled=True)]
    all_gather x1, blocking collectives: 42.1 us -> 38.1 us  [shards(): lax.all_gather(coefficients, ('kf', 'kc'), axis=0, tiled=True)]
  transfers between devices with their start and end apart: 1 -> 4, of which waited for: 0 -> 3; matrix products, arithmetic and copies ran while one was open for 1% -> 1% of each run, Pallas kernels for 0% -> 0%
where the time goes in v1:
time: 68.4 us; the launch traced here: 68 us
  blocking collectives  38.1 us (56%)
  waiting for transfers between devices  13.2 us (19%)
  local copies, waits for them, and re-layouts  7.97 us (12%)
  starting transfers between devices  7.37 us (11%)
  other arithmetic  0.86 us (1%)
    all_gather x1, blocking collectives, shards(): lax.all_gather(coefficients, ('kf', 'kc'), axis=0, tiled=True)  38.1 us
    all_to_all x1, starting transfers between devices, shards(): lax.all_to_all(outgoing, 'kf', split_axis=1, concat_axis=0, tiled=True)  7.31 us
    ppermute x3, waiting for transfers between devices, shards(): big = lax.ppermute(big, 'kc', out_arr)  7.27 us
    all_to_all x1, waiting for transfers between devices, shards(): lax.all_to_all(outgoing, 'kf', split_axis=1, concat_axis=0, tiled=True)  5.92 us
    unnamed x9, local copies, waits for them, and re-layouts  2.92 us
    gather x2, local copies, waits for them, and re-layouts, shards(): outgoing = jnp.take(kernel_coarse, columns, axis=1)  1.45 us
  transfers between devices with their start and end apart: 4, of which 3 were waited for; matrix products, arithmetic and copies ran while one was open for 1% of the time, Pallas kernels for 0%

profile of v1, /device:TPU:0, one launch (start us, length us, event | category | flops | bytes accessed | tf_op | source)
XLA Modules:
  0.0 68.0 jit_solution(12442896667675240025)
XLA Ops:
  0.0 0.7 copy-done.2
  0.7 0.1 reshape.90
  0.8 0.5 broadcast.59
  1.3 0.7 fusion.6
  2.0 0.1 mul.26
  2.1 0.1 add.96
  2.3 0.1 add.105
  2.4 0.1 add.98
  2.5 0.6 copy-done
  3.1 0.1 copy.19
  3.2 1.3 %gather_fusion = bf16[512,32]{1,0:T(8,128)(2,1)S(1)} fusion(bf16[32,256]{0,1:T(8,128)(2,1)S(1)} %copy.19, s32[1024]{0:T(1024)S(1)} %pad_clamp_fusion.1), kind=kCustom, calls=%fused_computation | custom fusion | bytes 67584 | tf_op jit(solution)/shard_map/jit(_take)/gather | solution.py:32
  4.6 0.1 copy.20
  4.7 0.7 %reshape.124 = bf16[8,2,1024]{2,1,0:T(2,128)(2,1)} reshape(bf16[8,32,64]{2,1,0:T(8,128)(2,1)S(1)} %fusion.7) | data formatting | bytes 65536
  5.4 7.3 %all-to-all-start = ((bf16[8,2,1024]{2,1,0:T(2,128)(2,1)}), bf16[8,2,1024]{2,1,0:T(2,128)(2,1)S(1)}, u32[]{:S(2)}, u32[]{:S(2)}) async-start(bf16[8,2,1024]{2,1,0:T(2,128)(2,1)} %reshape.124), calls=%async_computation | async-start | bytes 65536 | tf_op jit(solution)/shard_map/all_to_all | solution.py:33
  12.8 0.7 copy-done.1
  13.4 0.1 reshape.92
  13.5 5.9 %all-to-all-done = bf16[8,2,1024]{2,1,0:T(2,128)(2,1)S(1)} async-done(((bf16[8,2,1024]{2,1,0:T(2,128)(2,1)}), bf16[8,2,1024]{2,1,0:T(2,128)(2,1)S(1)}, u32[]{:S(2)}, u32[]{:S(2)}) %all-to-all-start) | async-done | bytes 32800 | tf_op jit(solution)/shard_map/all_to_all | solution.py:33
  19.4 0.1 reshape.125
  19.6 0.1 copy.21
  19.7 0.1 reshape.91
  19.8 0.1 convolution_convert_fusion.1
  20.0 0.1 copy.22
  20.1 0.1 compare_and_fusion.1
  20.2 3.6 %collective-permute-done = bf16[256,64]{1,0:T(8,128)(2,1)S(1)} collective-permute-done((bf16[256,64]{1,0:T(8,128)(2,1)S(1)}, bf16[256,64]{1,0:T(8,128)(2,1)S(1)}, u32[]{:S(2)}, u32[]{:S(2)}) %collective-permute-start) | collective-permute-done | bytes 32800 | tf_op jit(solution)/shard_map/ppermute | solution.py:41
  23.8 3.7 %collective-permute-done.1 = bf16[256,64]{1,0:T(8,128)(2,1)S(1)} collective-permute-done((bf16[256,64]{1,0:T(8,128)(2,1)S(1)}, bf16[256,64]{1,0:T(8,128)(2,1)S(1)}, u32[]{:S(2)}, u32[]{:S(2)}) %collective-permute-start.1) | collective-permute-done | bytes 32800 | tf_op jit(solution)/shard_map/ppermute | solution.py:41
  27.5 38.1 %all-gather = bf16[32,4,256]{2,1,0:T(4,128)(2,1)S(1)} all-gather(bf16[1,4,256]{2,1,0:T(4,128)(2,1)S(1)} %bitcast.28), channel_id=1, replica_groups=mesh['kf'=8,'kc'=4] {'kf','kc'}, dimensions={0}, use_global_device_ids=true | all-gather | bytes 67584 | tf_op jit(solution)/shard_map/all_gather | solution.py:25
  65.6 0.4 reshape.89
  66.0 0.2 concatenate.6
  66.2 0.1 constant_dynamic-slice_fusion
  66.3 0.6 gather_fusion.1
  66.9 0.3 convolution_convert_fusion
  67.2 0.8 %copy.25 = bf16[256,512]{1,0:T(8,128)(2,1)} copy(bf16[256,512]{0,1:T(8,128)(2,1)S(1)} %bitcast.24) | data formatting | bytes 524288 | tf_op jit(solution)/shard_map/convert_element_type | solution.py:53
  (16 shorter events, 0.3 us)
Async XLA Ops:
  0.0 0.7 copy-start.2
  2.4 0.7 %copy-start = (bf16[32,256]{1,0:T(8,128)(2,1)S(1)}, bf16[32,256]{1,0:T(8,128)(2,1)}, u32[]{:S(2)}) copy-start(bf16[32,256]{1,0:T(8,128)(2,1)} %param.3) | copy-start | bytes 49156
  5.4 14.0 %all-to-all-start = ((bf16[8,2,1024]{2,1,0:T(2,128)(2,1)}), bf16[8,2,1024]{2,1,0:T(2,128)(2,1)S(1)}, u32[]{:S(2)}, u32[]{:S(2)}) async-start(bf16[8,2,1024]{2,1,0:T(2,128)(2,1)} %reshape.124), calls=%async_computation | async-start | bytes 65536 | tf_op jit(solution)/shard_map/all_to_all | solution.py:33
  12.8 0.7 %copy-start.1 = (bf16[4,256]{1,0:T(4,128)(2,1)S(1)}, bf16[4,256]{1,0:T(4,128)(2,1)}, u32[]{:S(2)}) copy-start(bf16[4,256]{1,0:T(4,128)(2,1)} %param.4) | copy-start | bytes 6148
  20.1 3.7 %collective-permute-start = (bf16[256,64]{1,0:T(8,128)(2,1)S(1)}, bf16[256,64]{1,0:T(8,128)(2,1)S(1)}, u32[]{:S(2)}, u32[]{:S(2)}) collective-permute-start(bf16[256,64]{1,0:T(8,128)(2,1)S(1)} %copy.22), channel_id=1, source_target_pairs={{0,1},{1,2},{2,3},{3,0},{4,5},{5,6},{6,7},{7,4},{8,9},{9,10},{10,1... | collective-permute-start | bytes 98312 | tf_op jit(solution)/shard_map/ppermute | solution.py:41
  23.8 3.7 %collective-permute-start.1 = (bf16[256,64]{1,0:T(8,128)(2,1)S(1)}, bf16[256,64]{1,0:T(8,128)(2,1)S(1)}, u32[]{:S(2)}, u32[]{:S(2)}) collective-permute-start(bf16[256,64]{1,0:T(8,128)(2,1)S(1)} %collective-permute-done), channel_id=1, source_target_pairs={{0,1},{1,2},{2,3},{3,0},{4,5},{5,6},{6,7},{7,4},{8,9},{9,10},{10,1... | collective-permute-start | bytes 98312 | tf_op jit(solution)/shard_map/ppermute | solution.py:41
  27.5 38.5 %collective-permute-start.2 = (bf16[256,64]{1,0:T(8,128)(2,1)S(1)}, bf16[256,64]{1,0:T(8,128)(2,1)S(1)}, u32[]{:S(2)}, u32[]{:S(2)}) collective-permute-start(bf16[256,64]{1,0:T(8,128)(2,1)S(1)} %collective-permute-done.1), channel_id=1, source_target_pairs={{0,1},{1,2},{2,3},{3,0},{4,5},{5,6},{6,7},{7,4},{8,9},{9,10},{10,1... | collective-permute-start | bytes 98312 | tf_op jit(solution)/shard_map/ppermute | solution.py:41
